TPU v7x, 32 devices: a whole 2x2x4 slice. The times are simulated.
32 devices in a mesh: dp: 8 (over y, x, core), shard: 4 (over z).
Axes of the slice: x: 2, y: 2, z: 4, core: 2. Of those that a mesh axis runs over, the one named last changes fastest.
Arguments:
- momentum: float32 [4096, 7168], P('dp', 'shard'), may hold values from -6 to 6
- gradient: bfloat16 [4096, 7168], P('dp', 'shard'), may hold values from -120 to 120
Outputs:
- new_momentum: float32 [4096, 7168], P('dp', 'shard')
- update: float32 [4096, 7168], P('dp', 'shard')
All inputs are finite; a program needn't handle non-finite values.
Results may differ from a plain program's by a relative error of at most 0.0038.
The roundings to bfloat16 on the way count: a program that leaves them out, or rounds other values in their place, can miss the bound.
Values may be sent and summed in bfloat16 or wider, within the bound.
No kernel may reach another device: no remote copies, remote signals or barrier semaphores. Data moves between devices by JAX's collectives and lax.ppermute only.
A program may use at most 64 MiB of HBM per device.

v0:
```python
import math
import jax
import jax.numpy as jnp
from jax import lax
from jax.sharding import PartitionSpec as P

D = 7168
STEPS = 2
momentum_decay = 0.95
linear_term = 3.4445
cubic_term = -4.775
quintic_term = 2.0315


def apply_panel(gram_panel, right_side):
    return jnp.dot(gram_panel, right_side, preferred_element_type=jnp.float32)


def body(momentum, gradient):
    grad_full = gradient.astype(jnp.float32)
    new_momentum = momentum_decay * momentum + grad_full
    current = grad_full + momentum_decay * new_momentum
    for iteration in range(STEPS):
        matrix = current.astype(jnp.bfloat16)
        column_panel = lax.all_gather(matrix, "dp", axis=0, tiled=True)
        summed_part = lax.psum_scatter(
            lax.dot_general(
                matrix, column_panel, (((1,), (1,)), ((), ())), preferred_element_type=jnp.float32
            ),
            "shard",
            scatter_dimension=0,
            tiled=True,
        )
        gram_part = summed_part.astype(jnp.bfloat16)
        gram_panel = lax.all_gather(gram_part, "shard", axis=0, tiled=True)
        square_sum = lax.psum(jnp.sum(jnp.square(gram_part.astype(jnp.float32))), ("dp", "shard"))
        inverse_norm = lax.rsqrt(square_sum)
        root_scale = jnp.sqrt(inverse_norm)
        matrix_full = matrix.astype(jnp.float32)
        first_product = apply_panel(gram_panel, column_panel)
        mixture = (
            cubic_term * root_scale * matrix_full
            + quintic_term * root_scale * inverse_norm * first_product
        ).astype(jnp.bfloat16)
        second_product = apply_panel(gram_panel, lax.all_gather(mixture, "dp", axis=0, tiled=True))
        current = linear_term * root_scale * matrix_full + inverse_norm * second_product
    update = math.sqrt(D) * current
    return (new_momentum, update)


def solution(mesh):
    in_specs = (P("dp", "shard"), P("dp", "shard"))
    out_specs = (P("dp", "shard"), P("dp", "shard"))
    return jax.shard_map(body, mesh=mesh, in_specs=in_specs, out_specs=out_specs, check_vma=False)
```

profile of v0, /device:TPU:0, one launch (start us, length us, event | category | flops | bytes accessed | tf_op | source)
XLA Modules:
  0.0 889.7 jit_solution(13144774973173821033)
XLA Ops:
  7.2 5.7 fusion
  12.9 0.0 reduce-scatter.3.cloned.1.call-start
  13.0 83.7 %all-gather.7.cloned.1.call-done = bf16[4096,1792]{1,0:T(8,128)(2,1)} async-done(((bf16[512,1792]{1,0:T(8,128)(2,1)}), bf16[4096,1792]{1,0:T(8,128)(2,1)}) %all-gather.7.cloned.1.call-update) | async-done | bytes 14680080 | tf_op jit(solution)/shard_map/all_gather | solution.py:25
  96.7 13.5 %fusion.9 = f32[512,4096]{1,0:T(8,128)} fusion(bf16[512,1792]{1,0:T(8,128)(2,1)} %get-tuple-element.6, bf16[4096,1792]{1,0:T(8,128)(2,1)} %all-gather.7.cloned.1.call-done), kind=kOutput, calls=%fused_computation.17 | convolution fusion | flops 7516192768 | bytes 24903680 | tf_op jit(solution)/shard_map/dot_general | solution.py:27
  110.3 144.7 %reduce-scatter.3.cloned.1.call-done = f32[128,4096]{1,0:T(8,128)} async-done(((f32[512,4096]{1,0:T(8,128)}), f32[128,4096]{1,0:T(8,128)}) %reduce-scatter.3.cloned.1.call-update) | async-done | bytes 2097168 | tf_op jit(solution)/shard_map/reduce_scatter | solution.py:26
  255.0 3.7 multiply_reduce_fusion.1
  258.7 0.0 all-gather.11.cloned.1.call-start
  258.7 46.6 %psum.14 = f32[]{:T(128)} all-reduce(f32[]{:T(128)} %get-tuple-element.4), channel_id=1, replica_groups=mesh['dp'=8,'shard'=4] {'dp','shard'}, use_global_device_ids=true, to_apply=%region_2.0 | all-reduce | flops 1 | bytes 8 | tf_op jit(solution)/shard_map/psum | solution.py:36
  306.1 35.1 %all-gather.9.cloned.1.call-done = bf16[512,4096]{1,0:T(8,128)(2,1)} async-done(((bf16[128,4096]{1,0:T(8,128)(2,1)}), bf16[512,4096]{1,0:T(8,128)(2,1)}) %all-gather.9.cloned.1.call-update) | async-done | bytes 4194320 | tf_op jit(solution)/shard_map/all_gather | solution.py:35
  341.2 14.2 %fusion.4 = bf16[512,1792]{1,0:T(8,128)(2,1)} fusion(bf16[512,1792]{1,0:T(8,128)(2,1)S(1)} %copy-done, bf16[512,4096]{1,0:T(8,128)(2,1)} %all-gather.9.cloned.1.call-done, bf16[4096,1792]{1,0:T(8,128)(2,1)} %all-gather.7.cloned.1.call-done, f32[]{:T(128)S(6)} %mul.94, f32[]{:T(128)S(6)} %mul.90), kind=kOutput, calls=%fused_computation.10 | convolution fusion | flops 7520780288 | bytes 22544392 | tf_op jit(solution)/shard_map/dot_general | solution.py:16
  355.4 0.0 all-gather.13.cloned.1.call-start
  355.4 79.4 %all-gather.11.cloned.1.call-done = bf16[4096,1792]{1,0:T(8,128)(2,1)} async-done(((bf16[512,1792]{1,0:T(8,128)(2,1)}), bf16[4096,1792]{1,0:T(8,128)(2,1)}) %all-gather.11.cloned.1.call-update) | async-done | bytes 14680080 | tf_op jit(solution)/shard_map/all_gather | solution.py:45
  434.9 14.2 %fusion.2 = bf16[512,1792]{1,0:T(8,128)(2,1)} fusion(bf16[512,1792]{1,0:T(8,128)(2,1)S(1)} %copy-done, bf16[512,4096]{1,0:T(8,128)(2,1)} %all-gather.9.cloned.1.call-done, bf16[4096,1792]{1,0:T(8,128)(2,1)} %all-gather.11.cloned.1.call-done, f32[]{:T(128)S(6)} %rsqrt.6, f32[]{:T(128)S(6)} %mul.86), kind=kOutput, calls=%fused_computation.8 | convolution fusion | flops 7520780288 | bytes 22544392 | tf_op jit(solution)/shard_map/dot_general | solution.py:16
  449.1 0.2 reduce-scatter.5.cloned.1.call-start
  449.3 80.8 %all-gather.13.cloned.1.call-done = bf16[4096,1792]{1,0:T(8,128)(2,1)} async-done(((bf16[512,1792]{1,0:T(8,128)(2,1)}), bf16[4096,1792]{1,0:T(8,128)(2,1)}) %all-gather.13.cloned.1.call-update) | async-done | bytes 14680080 | tf_op jit(solution)/shard_map/all_gather | solution.py:25
  530.1 13.5 %fusion.10 = f32[512,4096]{1,0:T(8,128)} fusion(bf16[512,1792]{1,0:T(8,128)(2,1)} %fusion.2, bf16[4096,1792]{1,0:T(8,128)(2,1)} %all-gather.13.cloned.1.call-done), kind=kOutput, calls=%fused_computation.18 | convolution fusion | flops 7516192768 | bytes 24903680 | tf_op jit(solution)/shard_map/dot_general | solution.py:27
  543.7 0.0 all-gather.15.cloned.1.call-start
  543.7 144.7 %reduce-scatter.5.cloned.1.call-done = f32[128,4096]{1,0:T(8,128)} async-done(((f32[512,4096]{1,0:T(8,128)}), f32[128,4096]{1,0:T(8,128)}) %reduce-scatter.5.cloned.1.call-update) | async-done | bytes 2097168 | tf_op jit(solution)/shard_map/reduce_scatter | solution.py:26
  688.5 3.7 multiply_reduce_fusion
  692.2 46.6 %psum.15 = f32[]{:T(128)} all-reduce(f32[]{:T(128)} %get-tuple-element.2), channel_id=1, replica_groups=mesh['dp'=8,'shard'=4] {'dp','shard'}, use_global_device_ids=true, to_apply=%region_5.0 | all-reduce | flops 1 | bytes 8 | tf_op jit(solution)/shard_map/psum | solution.py:36
  739.5 35.1 %all-gather.15.cloned.1.call-done = bf16[512,4096]{1,0:T(8,128)(2,1)} async-done(((bf16[128,4096]{1,0:T(8,128)(2,1)}), bf16[512,4096]{1,0:T(8,128)(2,1)}) %all-gather.15.cloned.1.call-update) | async-done | bytes 4194320 | tf_op jit(solution)/shard_map/all_gather | solution.py:35
  774.6 14.2 %fusion.8 = bf16[512,1792]{1,0:T(8,128)(2,1)} fusion(bf16[512,1792]{1,0:T(8,128)(2,1)S(1)} %copy-done.1, bf16[512,4096]{1,0:T(8,128)(2,1)} %all-gather.15.cloned.1.call-done, bf16[4096,1792]{1,0:T(8,128)(2,1)} %all-gather.13.cloned.1.call-done, f32[]{:T(128)S(6)} %mul.106, f32[]{:T(128)S(6)} %mul.102), kind=kOutput, calls=%fused_computation.14 | convolution fusion | flops 7520780288 | bytes 22544392 | tf_op jit(solution)/shard_map/dot_general | solution.py:16
  788.8 79.5 %all-gather.17.cloned.1.call-done = bf16[4096,1792]{1,0:T(8,128)(2,1)} async-done(((bf16[512,1792]{1,0:T(8,128)(2,1)}), bf16[4096,1792]{1,0:T(8,128)(2,1)}) %all-gather.17.cloned.1.call-update) | async-done | bytes 14680080 | tf_op jit(solution)/shard_map/all_gather | solution.py:45
  868.3 14.5 %fusion.6 = f32[512,1792]{1,0:T(8,128)} fusion(bf16[512,1792]{1,0:T(8,128)(2,1)S(1)} %copy-done.1, bf16[512,4096]{1,0:T(8,128)(2,1)} %all-gather.15.cloned.1.call-done, bf16[4096,1792]{1,0:T(8,128)(2,1)} %all-gather.17.cloned.1.call-done, f32[]{:T(128)S(6)} %rsqrt.7, f32[]{:T(128)S(6)} %mul.98), kind=kOutput, calls=%fused_computation.12 | convolution fusion | flops 7520780288 | bytes 24379400 | tf_op jit(solution)/shard_map/dot_general | solution.py:16
  (15 shorter events, 0.3 us)
Async XLA Ops:
  7.2 89.5 %all-gather.7.cloned.1.call-start = ((), (), s32[]{:S(2)}) async-start(), calls=%async_computation.2 | async-start | bytes 16515072 | tf_op jit(solution)/shard_map/all_gather | solution.py:25
  12.9 242.1 %reduce-scatter.3.cloned.1.call-start = ((), (), s32[]{:S(2)}) async-start(), calls=%async_computation.3 | async-start | bytes 10485760 | tf_op jit(solution)/shard_map/reduce_scatter | solution.py:26
  110.2 230.9 %copy-start = (bf16[512,1792]{1,0:T(8,128)(2,1)S(1)}, bf16[512,1792]{1,0:T(8,128)(2,1)}, u32[]{:S(2)}) copy-start(bf16[512,1792]{1,0:T(8,128)(2,1)} %get-tuple-element.6) | copy-start | bytes 5505028
  110.2 230.9 %all-gather.9.cloned.1.call-start = ((), (), s32[]{:S(2)}) async-start(), calls=%async_computation.4 | async-start | bytes 5242880 | tf_op jit(solution)/shard_map/all_gather | solution.py:35
  258.7 176.2 %all-gather.11.cloned.1.call-start = ((), (), s32[]{:S(2)}) async-start(), calls=%async_computation.5 | async-start | bytes 16515072 | tf_op jit(solution)/shard_map/all_gather | solution.py:45
  355.4 174.7 %all-gather.13.cloned.1.call-start = ((), (), s32[]{:S(2)}) async-start(), calls=%async_computation.6 | async-start | bytes 16515072 | tf_op jit(solution)/shard_map/all_gather | solution.py:25
  449.1 239.3 %reduce-scatter.5.cloned.1.call-start = ((), (), s32[]{:S(2)}) async-start(), calls=%async_computation.7 | async-start | bytes 10485760 | tf_op jit(solution)/shard_map/reduce_scatter | solution.py:26
  543.7 230.9 %copy-start.1 = (bf16[512,1792]{1,0:T(8,128)(2,1)S(1)}, bf16[512,1792]{1,0:T(8,128)(2,1)}, u32[]{:S(2)}) copy-start(bf16[512,1792]{1,0:T(8,128)(2,1)} %fusion.2) | copy-start | bytes 5505028
  543.7 230.9 %all-gather.15.cloned.1.call-start = ((), (), s32[]{:S(2)}) async-start(), calls=%async_computation.8 | async-start | bytes 5242880 | tf_op jit(solution)/shard_map/all_gather | solution.py:35
  692.1 176.2 %all-gather.17.cloned.1.call-start = ((), (), s32[]{:S(2)}) async-start(), calls=%async_computation.9 | async-start | bytes 16515072 | tf_op jit(solution)/shard_map/all_gather | solution.py:45
Sparse Core Ops, SparseCore 0:
  13.0 83.5 all-gather.6
  110.3 144.6 reduce-scatter.2
  258.8 82.2 all-gather.8
  355.5 79.3 all-gather.10
  449.2 80.8 all-gather.12
  543.8 144.6 reduce-scatter.4
  692.3 82.2 all-gather.14
  789.0 79.3 all-gather.16
where the time goes:
time: 890 us
  waiting for transfers between devices  683 us (77%)
  blocking collectives  93.2 us (10%)
  matrix products  84.2 us (9%)
  between operations  15.6 us (2%)
  other arithmetic  13 us (1%)
    reduce_scatter x2, waiting for transfers between devices, body(): lax.psum_scatter(lax.dot_general(matrix, column_panel, (((1,), (1,)), (()...  289 us
    all_gather x2, waiting for transfers between devices, body(): column_panel = lax.all_gather(matrix, 'dp', axis=0, tiled=True)  164 us
    all_gather x2, waiting for transfers between devices, body(): lax.all_gather(mixture, 'dp', axis=0, tiled=True)  159 us
    psum x2, blocking collectives, body(): lax.psum(jnp.sum(jnp.square(gram_part.astype(jnp.float32))), ('dp', 'shar...  93.2 us
    all_gather x2, waiting for transfers between devices, body(): gram_panel = lax.all_gather(gram_part, 'shard', axis=0, tiled=True)  70.1 us
    dot_general x4, matrix products, apply_panel(): return jnp.dot(gram_panel, right_side, preferred_element_type=jnp.float32)  57.1 us
    dot_general x2, matrix products, body(): lax.dot_general(matrix, column_panel, (((1,), (1,)), ((), ())), preferred...  27.1 us
  transfers between devices with their start and end apart: 8, of which 8 were waited for; matrix products, arithmetic and copies ran while one was open for 0% of the time, Pallas kernels for 0%

commit v1 on v0

--- a/solution.py
+++ b/solution.py
@@ -32,7 +32,25 @@
             tiled=True,
         )
         gram_part = summed_part.astype(jnp.bfloat16)
-        gram_panel = lax.all_gather(gram_part, "shard", axis=0, tiled=True)
+        peers, index, rows = (lax.axis_size("shard"), lax.axis_index("shard"), gram_part.shape[0])
+        right = [(i, (i + 1) % peers) for i in range(peers)]
+        backward = [(i, (i - 1) % peers) for i in range(peers)]
+        gram_panel = jnp.zeros(
+            (*gram_part.shape[:0], peers * rows, *gram_part.shape[0 + 1 :]), gram_part.dtype
+        )
+        gram_panel = lax.dynamic_update_slice_in_dim(gram_panel, gram_part, index * rows, axis=0)
+        from_left = from_right = gram_part
+        halfway = peers // 2
+        for step in range(1, halfway + 1):
+            from_left = lax.ppermute(from_left, "shard", right)
+            gram_panel = lax.dynamic_update_slice_in_dim(
+                gram_panel, from_left, (index - step) % peers * rows, axis=0
+            )
+            if step < peers - halfway:
+                from_right = lax.ppermute(from_right, "shard", backward)
+                gram_panel = lax.dynamic_update_slice_in_dim(
+                    gram_panel, from_right, (index + step) % peers * rows, axis=0
+                )
         square_sum = lax.psum(jnp.sum(jnp.square(gram_part.astype(jnp.float32))), ("dp", "shard"))
         inverse_norm = lax.rsqrt(square_sum)
         root_scale = jnp.sqrt(inverse_norm)

time: 890 us -> 927 us (1.042)
  starting transfers between devices: 0.51 us -> 50.6 us
  waiting for transfers between devices: 683 us -> 663 us
  local copies, waits for them, and re-layouts: 0.01 us -> 18.9 us
  blocking collectives: 93.2 us -> 82.9 us
    all_gather x2 -> x0, waiting for transfers between devices: 70.1 us -> none  [body(): gram_panel = lax.all_gather(gram_part, 'shard', axis=0, tiled=True)]
    ppermute x0 -> x6, starting transfers between devices: none -> 50.1 us  [the longest x4 44.6 us: body(): from_left = lax.ppermute(from_left, 'shard', right)]
    ppermute x0 -> x6, waiting for transfers between devices: none -> 48.3 us  [the longest x4 48.3 us: body(): from_left = lax.ppermute(from_left, 'shard', right)]
    dynamic_update_slice x0 -> x8, local copies, waits for them, and re-layouts: none -> 14 us  [the longest x4 9.23 us: body(): lax.dynamic_update_slice_in_dim(gram_panel, from_left, (index - step) % p...]
    psum x2, blocking collectives: 93.2 us -> 82.9 us  [body(): lax.psum(jnp.sum(jnp.square(gram_part.astype(jnp.float32))), ('dp', 'shar...]
  transfers between devices with their start and end apart: 8 -> 12, of which waited for: 8 -> 8; matrix products, arithmetic and copies ran while one was open for 0% -> 1% of each run, Pallas kernels for 0% -> 0%
where the time goes in v1:
time: 927 us; the launch traced here: 926 us
  waiting for transfers between devices  663 us (72%)
  matrix products  84.3 us (9%)
  blocking collectives  82.9 us (9%)
  starting transfers between devices  50.6 us (5%)
  local copies, waits for them, and re-layouts  18.9 us (2%)
  between operations  15.6 us (2%)
  other arithmetic  11.2 us (1%)
    reduce_scatter x2, waiting for transfers between devices, body(): lax.psum_scatter(lax.dot_general(matrix, column_panel, (((1,), (1,)), (()...  289 us
    all_gather x2, waiting for transfers between devices, body(): column_panel = lax.all_gather(matrix, 'dp', axis=0, tiled=True)  164 us
    all_gather x2, waiting for transfers between devices, body(): lax.all_gather(mixture, 'dp', axis=0, tiled=True)  161 us
    psum x2, blocking collectives, body(): lax.psum(jnp.sum(jnp.square(gram_part.astype(jnp.float32))), ('dp', 'shar...  82.9 us
    dot_general x4, matrix products, apply_panel(): return jnp.dot(gram_panel, right_side, preferred_element_type=jnp.float32)  57.2 us
    ppermute x4, waiting for transfers between devices, body(): from_left = lax.ppermute(from_left, 'shard', right)  48.3 us
    ppermute x4, starting transfers between devices, body(): from_left = lax.ppermute(from_left, 'shard', right)  44.6 us
    dot_general x2, matrix products, body(): lax.dot_general(matrix, column_panel, (((1,), (1,)), ((), ())), preferred...  27.1 us
  transfers between devices with their start and end apart: 12, of which 8 were waited for; matrix products, arithmetic and copies ran while one was open for 1% of the time, Pallas kernels for 0%

profile of v1, /device:TPU:0, one launch (start us, length us, event | category | flops | bytes accessed | tf_op | source)
XLA Modules:
  0.0 926.5 jit_solution(4461363610900703909)
XLA Ops:
  7.2 5.7 fusion
  13.0 83.7 %all-gather.5.cloned.1.call-done = bf16[4096,1792]{1,0:T(8,128)(2,1)} async-done(((bf16[512,1792]{1,0:T(8,128)(2,1)}), bf16[4096,1792]{1,0:T(8,128)(2,1)}) %all-gather.5.cloned.1.call-update) | async-done | bytes 14680080 | tf_op jit(solution)/shard_map/all_gather | solution.py:25
  96.7 13.5 %fusion.9 = f32[512,4096]{1,0:T(8,128)} fusion(bf16[512,1792]{1,0:T(8,128)(2,1)} %get-tuple-element.6, bf16[4096,1792]{1,0:T(8,128)(2,1)} %all-gather.5.cloned.1.call-done), kind=kOutput, calls=%fused_computation.25 | convolution fusion | flops 7516192768 | bytes 24903680 | tf_op jit(solution)/shard_map/dot_general | solution.py:27
  110.3 144.7 %reduce-scatter.3.cloned.1.call-done = f32[128,4096]{1,0:T(8,128)} async-done(((f32[512,4096]{1,0:T(8,128)}), f32[128,4096]{1,0:T(8,128)}) %reduce-scatter.3.cloned.1.call-update) | async-done | bytes 2097168 | tf_op jit(solution)/shard_map/reduce_scatter | solution.py:26
  255.0 2.8 multiply_reduce_fusion.1
  258.8 2.8 collective-permute-start.1
  261.6 24.2 %collective-permute-done = bf16[128,4096]{1,0:T(8,128)(2,1)} collective-permute-done((bf16[128,4096]{1,0:T(8,128)(2,1)S(1)}, bf16[128,4096]{1,0:T(8,128)(2,1)}, u32[]{:S(2)}, u32[]{:S(2)}) %collective-permute-start) | collective-permute-done | bytes 1048608 | tf_op jit(solution)/shard_map/ppermute | solution.py:45
  285.7 21.3 %collective-permute-start.2 = (bf16[128,4096]{1,0:T(8,128)(2,1)}, bf16[128,4096]{1,0:T(8,128)(2,1)}, u32[]{:S(2)}, u32[]{:S(2)}) collective-permute-start(bf16[128,4096]{1,0:T(8,128)(2,1)} %collective-permute-done), channel_id=1, source_target_pairs={{0,1},{1,2},{2,3},{3,0},{4,5},{5,6},{6,7},{7,4},{8,9},{9,10},{10,1... | collective-permute-start | bytes 3145736 | tf_op jit(solution)/shard_map/ppermute | solution.py:45
  309.6 41.5 %psum.14 = f32[]{:T(128)} all-reduce(f32[]{:T(128)} %get-tuple-element.4), channel_id=1, replica_groups=mesh['dp'=8,'shard'=4] {'dp','shard'}, use_global_device_ids=true, to_apply=%region_2.3 | all-reduce | flops 1 | bytes 8 | tf_op jit(solution)/shard_map/psum | solution.py:54
  351.7 2.3 constant_dynamic-update-slice_fusion.6
  358.6 14.2 %fusion.4 = bf16[512,1792]{1,0:T(8,128)(2,1)} fusion(bf16[512,1792]{1,0:T(8,128)(2,1)S(1)} %copy-done, bf16[512,4096]{1,0:T(8,128)(2,1)} %constant_dynamic-update-slice_fusion.4, bf16[4096,1792]{1,0:T(8,128)(2,1)} %all-gather.5.cloned.1.call-done, f32[]{:T(128)S(6)} %mul.114, f32[]{:T(128)S(6)} %mul.110), kind=kOutput, calls=%fused_computation.10 | convolution fusion | flops 7520780288 | bytes 22544392 | tf_op jit(solution)/shard_map/dot_general | solution.py:16
  373.0 80.3 %all-gather.7.cloned.1.call-done = bf16[4096,1792]{1,0:T(8,128)(2,1)} async-done(((bf16[512,1792]{1,0:T(8,128)(2,1)}), bf16[4096,1792]{1,0:T(8,128)(2,1)}) %all-gather.7.cloned.1.call-update) | async-done | bytes 14680080 | tf_op jit(solution)/shard_map/all_gather | solution.py:63
  453.2 14.2 %fusion.2 = bf16[512,1792]{1,0:T(8,128)(2,1)} fusion(bf16[512,1792]{1,0:T(8,128)(2,1)S(1)} %copy-done, bf16[512,4096]{1,0:T(8,128)(2,1)} %constant_dynamic-update-slice_fusion.4, bf16[4096,1792]{1,0:T(8,128)(2,1)} %all-gather.7.cloned.1.call-done, f32[]{:T(128)S(6)} %rsqrt.6, f32[]{:T(128)S(6)} %mul.102), kind=kOutput, calls=%fused_computation.8 | convolution fusion | flops 7520780288 | bytes 22544392 | tf_op jit(solution)/shard_map/dot_general | solution.py:16
  467.7 80.8 %all-gather.9.cloned.1.call-done = bf16[4096,1792]{1,0:T(8,128)(2,1)} async-done(((bf16[512,1792]{1,0:T(8,128)(2,1)}), bf16[4096,1792]{1,0:T(8,128)(2,1)}) %all-gather.9.cloned.1.call-update) | async-done | bytes 14680080 | tf_op jit(solution)/shard_map/all_gather | solution.py:25
  548.5 13.5 %fusion.10 = f32[512,4096]{1,0:T(8,128)} fusion(bf16[512,1792]{1,0:T(8,128)(2,1)} %fusion.2, bf16[4096,1792]{1,0:T(8,128)(2,1)} %all-gather.9.cloned.1.call-done), kind=kOutput, calls=%fused_computation.26 | convolution fusion | flops 7516192768 | bytes 24903680 | tf_op jit(solution)/shard_map/dot_general | solution.py:27
  562.1 144.7 %reduce-scatter.5.cloned.1.call-done = f32[128,4096]{1,0:T(8,128)} async-done(((f32[512,4096]{1,0:T(8,128)}), f32[128,4096]{1,0:T(8,128)}) %reduce-scatter.5.cloned.1.call-update) | async-done | bytes 2097168 | tf_op jit(solution)/shard_map/reduce_scatter | solution.py:26
  706.8 2.8 multiply_reduce_fusion
  710.7 2.8 collective-permute-start.4
  713.4 24.2 %collective-permute-done.3 = bf16[128,4096]{1,0:T(8,128)(2,1)} collective-permute-done((bf16[128,4096]{1,0:T(8,128)(2,1)S(1)}, bf16[128,4096]{1,0:T(8,128)(2,1)}, u32[]{:S(2)}, u32[]{:S(2)}) %collective-permute-start.3) | collective-permute-done | bytes 1048608 | tf_op jit(solution)/shard_map/ppermute | solution.py:45
  737.6 21.2 %collective-permute-start.5 = (bf16[128,4096]{1,0:T(8,128)(2,1)}, bf16[128,4096]{1,0:T(8,128)(2,1)}, u32[]{:S(2)}, u32[]{:S(2)}) collective-permute-start(bf16[128,4096]{1,0:T(8,128)(2,1)} %collective-permute-done.3), channel_id=1, source_target_pairs={{0,1},{1,2},{2,3},{3,0},{4,5},{5,6},{6,7},{7,4},{8,9},{9,10},{10,1... | collective-permute-start | bytes 3145736 | tf_op jit(solution)/shard_map/ppermute | solution.py:45
  761.4 41.5 %psum.15 = f32[]{:T(128)} all-reduce(f32[]{:T(128)} %get-tuple-element.2), channel_id=1, replica_groups=mesh['dp'=8,'shard'=4] {'dp','shard'}, use_global_device_ids=true, to_apply=%region_5.6 | all-reduce | flops 1 | bytes 8 | tf_op jit(solution)/shard_map/psum | solution.py:54
  810.5 14.2 %fusion.8 = bf16[512,1792]{1,0:T(8,128)(2,1)} fusion(bf16[512,1792]{1,0:T(8,128)(2,1)S(1)} %copy-done.3, bf16[512,4096]{1,0:T(8,128)(2,1)} %constant_dynamic-update-slice_fusion, bf16[4096,1792]{1,0:T(8,128)(2,1)} %all-gather.9.cloned.1.call-done, f32[]{:T(128)S(6)} %mul.126, f32[]{:T(128)S(6)} %mul.122), kind=kOutput, calls=%fused_computation.14 | convolution fusion | flops 7520780288 | bytes 22544392 | tf_op jit(solution)/shard_map/dot_general | solution.py:16
  824.7 80.3 %all-gather.11.cloned.1.call-done = bf16[4096,1792]{1,0:T(8,128)(2,1)} async-done(((bf16[512,1792]{1,0:T(8,128)(2,1)}), bf16[4096,1792]{1,0:T(8,128)(2,1)}) %all-gather.11.cloned.1.call-update) | async-done | bytes 14680080 | tf_op jit(solution)/shard_map/all_gather | solution.py:63
  905.1 14.5 %fusion.6 = f32[512,1792]{1,0:T(8,128)} fusion(bf16[512,1792]{1,0:T(8,128)(2,1)S(1)} %copy-done.3, bf16[512,4096]{1,0:T(8,128)(2,1)} %constant_dynamic-update-slice_fusion, bf16[4096,1792]{1,0:T(8,128)(2,1)} %all-gather.11.cloned.1.call-done, f32[]{:T(128)S(6)} %rsqrt.7, f32[]{:T(128)S(6)} %mul.118), kind=kOutput, calls=%fused_computation.12 | convolution fusion | flops 7520780288 | bytes 24379400 | tf_op jit(solution)/shard_map/dot_general | solution.py:16
  (35 shorter events, 19.3 us)
Async XLA Ops:
  7.2 89.5 %all-gather.5.cloned.1.call-start = ((), (), s32[]{:S(2)}) async-start(), calls=%async_computation.2 | async-start | bytes 16515072 | tf_op jit(solution)/shard_map/all_gather | solution.py:25
  12.9 242.1 %reduce-scatter.3.cloned.1.call-start = ((), (), s32[]{:S(2)}) async-start(), calls=%async_computation.3 | async-start | bytes 10485760 | tf_op jit(solution)/shard_map/reduce_scatter | solution.py:26
  110.2 343.0 %all-gather.7.cloned.1.call-start = ((), (), s32[]{:S(2)}) async-start(), calls=%async_computation.4 | async-start | bytes 16515072 | tf_op jit(solution)/shard_map/all_gather | solution.py:63
  257.8 28.0 %collective-permute-start = (bf16[128,4096]{1,0:T(8,128)(2,1)S(1)}, bf16[128,4096]{1,0:T(8,128)(2,1)}, u32[]{:S(2)}, u32[]{:S(2)}) collective-permute-start(bf16[128,4096]{1,0:T(8,128)(2,1)S(1)} %get-tuple-element.5), channel_id=1, source_target_pairs={{0,1},{1,2},{2,3},{3,0},{4,5},{5,6},{6,7},{7,4},{8,9},{9,10},{10,1... | collective-permute-start | bytes 3145736 | tf_op jit(solution)/shard_map/ppermute | solution.py:45
  258.8 95.2 %collective-permute-start.1 = (bf16[128,4096]{1,0:T(8,128)(2,1)S(1)}, bf16[128,4096]{1,0:T(8,128)(2,1)}, u32[]{:S(2)}, u32[]{:S(2)}) collective-permute-start(bf16[128,4096]{1,0:T(8,128)(2,1)S(1)} %get-tuple-element.5), channel_id=1, source_target_pairs={{0,3},{1,0},{2,1},{3,2},{4,7},{5,4},{6,5},{7,6},{8,11},{9,8},{10,9... | collective-permute-start | bytes 3145736 | tf_op jit(solution)/shard_map/ppermute | solution.py:50
  285.7 70.6 %collective-permute-start.2 = (bf16[128,4096]{1,0:T(8,128)(2,1)}, bf16[128,4096]{1,0:T(8,128)(2,1)}, u32[]{:S(2)}, u32[]{:S(2)}) collective-permute-start(bf16[128,4096]{1,0:T(8,128)(2,1)} %collective-permute-done), channel_id=1, source_target_pairs={{0,1},{1,2},{2,3},{3,0},{4,5},{5,6},{6,7},{7,4},{8,9},{9,10},{10,1... | collective-permute-start | bytes 3145736 | tf_op jit(solution)/shard_map/ppermute | solution.py:45
  307.6 2.0 copy-start.2
  309.6 49.1 %copy-start = (bf16[512,1792]{1,0:T(8,128)(2,1)S(1)}, bf16[512,1792]{1,0:T(8,128)(2,1)}, u32[]{:S(2)}) copy-start(bf16[512,1792]{1,0:T(8,128)(2,1)} %get-tuple-element.6) | copy-start | bytes 5505028
  372.9 175.6 %all-gather.9.cloned.1.call-start = ((), (), s32[]{:S(2)}) async-start(), calls=%async_computation.5 | async-start | bytes 16515072 | tf_op jit(solution)/shard_map/all_gather | solution.py:25
  467.5 239.3 %reduce-scatter.5.cloned.1.call-start = ((), (), s32[]{:S(2)}) async-start(), calls=%async_computation.6 | async-start | bytes 10485760 | tf_op jit(solution)/shard_map/reduce_scatter | solution.py:26
  562.1 343.0 %all-gather.11.cloned.1.call-start = ((), (), s32[]{:S(2)}) async-start(), calls=%async_computation.7 | async-start | bytes 16515072 | tf_op jit(solution)/shard_map/all_gather | solution.py:63
  709.6 28.0 %collective-permute-start.3 = (bf16[128,4096]{1,0:T(8,128)(2,1)S(1)}, bf16[128,4096]{1,0:T(8,128)(2,1)}, u32[]{:S(2)}, u32[]{:S(2)}) collective-permute-start(bf16[128,4096]{1,0:T(8,128)(2,1)S(1)} %get-tuple-element.3), channel_id=1, source_target_pairs={{0,1},{1,2},{2,3},{3,0},{4,5},{5,6},{6,7},{7,4},{8,9},{9,10},{10,1... | collective-permute-start | bytes 3145736 | tf_op jit(solution)/shard_map/ppermute | solution.py:45
  710.7 95.2 %collective-permute-start.4 = (bf16[128,4096]{1,0:T(8,128)(2,1)S(1)}, bf16[128,4096]{1,0:T(8,128)(2,1)}, u32[]{:S(2)}, u32[]{:S(2)}) collective-permute-start(bf16[128,4096]{1,0:T(8,128)(2,1)S(1)} %get-tuple-element.3), channel_id=1, source_target_pairs={{0,3},{1,0},{2,1},{3,2},{4,7},{5,4},{6,5},{7,6},{8,11},{9,8},{10,9... | collective-permute-start | bytes 3145736 | tf_op jit(solution)/shard_map/ppermute | solution.py:50
  737.6 70.6 %collective-permute-start.5 = (bf16[128,4096]{1,0:T(8,128)(2,1)}, bf16[128,4096]{1,0:T(8,128)(2,1)}, u32[]{:S(2)}, u32[]{:S(2)}) collective-permute-start(bf16[128,4096]{1,0:T(8,128)(2,1)} %collective-permute-done.3), channel_id=1, source_target_pairs={{0,1},{1,2},{2,3},{3,0},{4,5},{5,6},{6,7},{7,4},{8,9},{9,10},{10,1... | collective-permute-start | bytes 3145736 | tf_op jit(solution)/shard_map/ppermute | solution.py:45
  759.4 2.0 copy-start.1
  761.4 49.1 %copy-start.3 = (bf16[512,1792]{1,0:T(8,128)(2,1)S(1)}, bf16[512,1792]{1,0:T(8,128)(2,1)}, u32[]{:S(2)}) copy-start(bf16[512,1792]{1,0:T(8,128)(2,1)} %fusion.2) | copy-start | bytes 5505028
Sparse Core Ops, SparseCore 0:
  13.0 83.5 all-gather.4
  110.3 144.6 reduce-scatter.2
  373.0 80.1 all-gather.6
  467.6 80.8 all-gather.8
  562.2 144.6 reduce-scatter.4
  824.9 80.1 all-gather.10
